TPU v7x, 32 devices: a whole 2x2x4 slice. The times are simulated.
32 devices in a mesh: tower: 2 (over x), dp: 16 (over z, y, core).
Axes of the slice: x: 2, y: 2, z: 4, core: 2. Of those that a mesh axis runs over, the one named last changes fastest.
Arguments:
- tokens: bfloat16 [2, 128, 77, 768], P('tower', 'dp'), as said below
- lengths: int32 [128], P('dp'), may hold values from 5 to 77, as said below
- ln1_gain: bfloat16 [2, 768], P('tower', 'dp'), as said below
- ln1_bias: bfloat16 [2, 768], P('tower', 'dp'), as said below
- qkv_weight: bfloat16 [2, 768, 3, 768], P('tower', 'dp'), as said below
- qv_bias: bfloat16 [2, 2, 768], P('tower', None, 'dp'), as said below
- out_weight: bfloat16 [2, 768, 768], P('tower', 'dp'), as said below
- out_bias: bfloat16 [2, 768], P('tower', 'dp'), as said below
- ln2_gain: bfloat16 [2, 768], P('tower', 'dp'), as said below
- ln2_bias: bfloat16 [2, 768], P('tower', 'dp'), as said below
- fc_weight: bfloat16 [2, 768, 3072], P('tower', 'dp'), as said below
- fc_bias: bfloat16 [2, 3072], P('tower', 'dp'), as said below
- down_weight: bfloat16 [2, 3072, 768], P('tower', 'dp'), as said below
- down_bias: bfloat16 [2, 768], P('tower', 'dp'), as said below
- final_gain: bfloat16 [2, 768], P('tower', 'dp'), as said below
- final_bias: bfloat16 [2, 768], P('tower', 'dp'), as said below
- embed_weight: bfloat16 [2, 768, 512], P('tower', 'dp'), as said below
- logit_scale: float32 [1], replicated, may hold values from 3.4 to 4.1
Outputs:
- block_out: bfloat16 [2, 128, 77, 768], P('tower', 'dp')
- tokens_grad: float32 [2, 128, 77, 768], P('tower', 'dp')
- loss: float32 [1], replicated
- ln1_gain_grad: float32 [2, 768], P('tower', 'dp')
- ln1_bias_grad: float32 [2, 768], P('tower', 'dp')
- qkv_weight_grad: float32 [2, 768, 3, 768], P('tower', 'dp')
- qv_bias_grad: float32 [2, 2, 768], P('tower', None, 'dp')
- out_weight_grad: float32 [2, 768, 768], P('tower', 'dp')
- out_bias_grad: float32 [2, 768], P('tower', 'dp')
- ln2_gain_grad: float32 [2, 768], P('tower', 'dp')
- ln2_bias_grad: float32 [2, 768], P('tower', 'dp')
- fc_weight_grad: float32 [2, 768, 3072], P('tower', 'dp')
- fc_bias_grad: float32 [2, 3072], P('tower', 'dp')
- down_weight_grad: float32 [2, 3072, 768], P('tower', 'dp')
- down_bias_grad: float32 [2, 768], P('tower', 'dp')
- final_gain_grad: float32 [2, 768], P('tower', 'dp')
- final_bias_grad: float32 [2, 768], P('tower', 'dp')
- embed_weight_grad: float32 [2, 768, 512], P('tower', 'dp')
- logit_scale_grad: float32 [1], replicated
Inputs may be any that keep to these rules, and one draw needn't show every extreme that they name: `tokens`: image slot zero from row 50 on; text slot zero from feature 512 on. `lengths`: device 0 of dp holds a caption of 77 slots and one of 5. `ln1_gain`: text slot zero from feature 512 on. `ln1_bias`: text slot zero from feature 512 on. `qkv_weight`: text slot zero outside its first 512 rows and first 512 columns of each third. `qv_bias`: text slot zero from feature 512 on. `out_weight`: text slot zero outside its leading 512 x 512 block. `out_bias`: text slot zero from feature 512 on. `ln2_gain`: text slot zero from feature 512 on. `ln2_bias`: text slot zero from feature 512 on. `fc_weight`: text slot zero outside its leading 512 x 2048 block. `fc_bias`: text slot zero from unit 2048 on. `down_weight`: text slot zero outside its leading 2048 x 512 block. `down_bias`: text slot zero from feature 512 on. `final_gain`: text slot zero from feature 512 on. `final_bias`: text slot zero from feature 512 on. `embed_weight`: text slot zero from row 512 on.
All inputs are finite; a program needn't handle non-finite values.
Results may differ from a plain program's by a relative error of at most 0.02.
The roundings to bfloat16 on the way count: a program that leaves them out, or rounds other values in their place, can miss the bound.
Values may be sent and summed in bfloat16 or wider, within the bound.
No kernel may reach another device: no remote copies, remote signals or barrier semaphores. Data moves between devices by JAX's collectives and lax.ppermute only.
A program may use at most 192 MiB of HBM per device.

v0:
```python
import jax
import jax.numpy as jnp
from jax import lax
from jax.sharding import PartitionSpec as P

DI = 768
DT = 512
HD = 64
IMG_ROWS = 50
EPS = 1e-05
NORM_EPS = 1e-06
GELU_K = 1.702
NEG_FILL = -1e30


def swapped(block, axis, stride):
    count = lax.axis_size(axis)
    route = []
    for low in range(count):
        high = low | 1 << stride
        if high != low and high < count:
            route += [(low, high), (high, low)]
    return lax.ppermute(block, axis, route)


def masked_norm(values, norm_gain, norm_bias, col_keep, width_real):
    row_mean = jnp.sum(values * col_keep, axis=-1, keepdims=True) / width_real
    centred = (values - row_mean) * col_keep
    row_var = jnp.sum(centred * centred, axis=-1, keepdims=True) / width_real
    inv_std = lax.rsqrt(row_var + EPS)
    normed = centred * inv_std
    return (normed * norm_gain + norm_bias, normed, inv_std)


def masked_norm_back(grad_out, norm_gain, normed, inv_std, col_keep, width_real):
    grad_normed = grad_out * norm_gain
    mean_grad = jnp.sum(grad_normed, axis=-1, keepdims=True) / width_real
    mean_cross = jnp.sum(grad_normed * normed, axis=-1, keepdims=True) / width_real
    grad_in = col_keep * inv_std * (grad_normed - mean_grad - normed * mean_cross)
    return (grad_in, jnp.sum(grad_out * normed, axis=0), jnp.sum(grad_out, axis=0))


def contract_rows(left_op, right_op):
    return lax.dot_general(
        left_op, right_op, (((0,), (0,)), ((), ())), preferred_element_type=jnp.float32
    )


def contract_cols(left_op, right_op):
    return lax.dot_general(
        left_op, right_op, (((1,), (1,)), ((), ())), preferred_element_type=jnp.float32
    )


def column_sum(values):
    return jnp.sum(values, axis=0, dtype=jnp.float32)


def body(
    tokens,
    lengths,
    ln1_gain,
    ln1_bias,
    qkv_weight,
    qv_bias,
    out_weight,
    out_bias,
    ln2_gain,
    ln2_bias,
    fc_weight,
    fc_bias,
    down_weight,
    down_bias,
    final_gain,
    final_bias,
    embed_weight,
    logit_scale,
):
    f32 = jnp.float32
    bf16 = jnp.bfloat16
    tower_index = lax.axis_index("tower")
    dp_index = lax.axis_index("dp")
    dp_count = lax.axis_size("dp")
    samples, seq_rows, width_all = (tokens.shape[1], tokens.shape[2], tokens.shape[3])
    head_count = width_all // HD
    sample_total = samples * dp_count
    flat_rows = samples * seq_rows
    is_text = tower_index == 1
    width_int = jnp.where(is_text, DT, DI)
    width_real = width_int.astype(f32)
    col_keep = (lax.broadcasted_iota(jnp.int32, (width_all,), 0) < width_int).astype(f32)
    seq_lens = jnp.where(is_text, lengths, IMG_ROWS)
    positions = lax.broadcasted_iota(jnp.int32, (samples, seq_rows), 1)
    row_keep = (positions < seq_lens[:, None]).astype(f32).reshape(flat_rows, 1)
    query_pos = lax.broadcasted_iota(jnp.int32, (seq_rows, seq_rows), 0)
    key_pos = lax.broadcasted_iota(jnp.int32, (seq_rows, seq_rows), 1)
    allowed = (key_pos[None] < seq_lens[:, None, None]) & (
        jnp.logical_not(is_text) | (key_pos <= query_pos)
    )[None]
    pool_pos = jnp.where(is_text, lengths - 1, 0)
    pool_hot = (positions == pool_pos[:, None]).astype(f32)
    score_mult = float(HD) ** (-0.5)
    gathered = (
        lax.all_gather(ln1_gain[0], "dp", axis=0, tiled=True),
        lax.all_gather(ln1_bias[0], "dp", axis=0, tiled=True),
        lax.all_gather(qkv_weight[0], "dp", axis=0, tiled=True),
        lax.all_gather(qv_bias[0], "dp", axis=1, tiled=True),
        lax.all_gather(out_weight[0], "dp", axis=0, tiled=True),
        lax.all_gather(out_bias[0], "dp", axis=0, tiled=True),
        lax.all_gather(ln2_gain[0], "dp", axis=0, tiled=True),
        lax.all_gather(ln2_bias[0], "dp", axis=0, tiled=True),
        lax.all_gather(fc_weight[0], "dp", axis=0, tiled=True),
        lax.all_gather(fc_bias[0], "dp", axis=0, tiled=True),
        lax.all_gather(down_weight[0], "dp", axis=0, tiled=True),
        lax.all_gather(down_bias[0], "dp", axis=0, tiled=True),
        lax.all_gather(final_gain[0], "dp", axis=0, tiled=True),
        lax.all_gather(final_bias[0], "dp", axis=0, tiled=True),
        lax.all_gather(embed_weight[0], "dp", axis=0, tiled=True),
    )
    (
        gain_one,
        bias_one,
        w_qkv,
        b_qv,
        w_out,
        b_out,
        gain_two,
        bias_two,
        w_fc,
        b_fc,
        w_down,
        b_down,
        gain_final,
        bias_final,
        w_embed,
    ) = gathered
    stream = tokens[0].astype(f32).reshape(flat_rows, width_all)
    normed_h1, norm_one, inv_one = masked_norm(
        stream, gain_one.astype(f32), bias_one.astype(f32), col_keep, width_real
    )
    normed_one = normed_h1.astype(bf16)
    qkv_bias = jnp.concatenate(
        [b_qv[0].astype(f32), jnp.zeros((width_all,), f32), b_qv[1].astype(f32)]
    )
    qkv_flat = (
        jnp.dot(normed_one, w_qkv.reshape(width_all, 3 * width_all), preferred_element_type=f32)
        + qkv_bias
    )
    qkv_low = qkv_flat.astype(bf16).reshape(samples, seq_rows, 3, head_count, HD)
    query_all = qkv_low[:, :, 0]
    key_all = qkv_low[:, :, 1]
    value_all = qkv_low[:, :, 2]

    def masked_scores():
        raw = (
            jnp.einsum("sqhd,skhd->shqk", query_all, key_all, preferred_element_type=f32)
            * score_mult
        )
        return jnp.where(allowed[:, None], raw, NEG_FILL)

    scores = masked_scores()
    row_top = jnp.max(scores, axis=-1, keepdims=True)
    exp_terms = jnp.exp(scores - row_top)
    exp_sum = jnp.sum(exp_terms, axis=-1, keepdims=True)
    log_total = row_top + jnp.log(exp_sum)
    attn_probs = (exp_terms / exp_sum).astype(bf16)
    head_mix = jnp.einsum("shqk,skhd->sqhd", attn_probs, value_all, preferred_element_type=f32)
    head_mix_low = head_mix.astype(bf16).reshape(flat_rows, width_all)
    attn_out = jnp.dot(head_mix_low, w_out, preferred_element_type=f32) + b_out.astype(f32)
    middle = stream + attn_out
    normed_h2, norm_two, inv_two = masked_norm(
        middle, gain_two.astype(f32), bias_two.astype(f32), col_keep, width_real
    )
    normed_two = normed_h2.astype(bf16)
    hidden_pre = jnp.dot(normed_two, w_fc, preferred_element_type=f32) + b_fc.astype(f32)
    gate_sig = jax.nn.sigmoid(GELU_K * hidden_pre)
    act_low = (hidden_pre * gate_sig).astype(bf16)
    branch = jnp.dot(act_low, w_down, preferred_element_type=f32) + b_down.astype(f32)
    block_rows = row_keep * (middle + branch)
    block_out = block_rows.astype(bf16).reshape(1, samples, seq_rows, width_all)
    block_three = block_rows.reshape(samples, seq_rows, width_all)
    pooled = jnp.take_along_axis(block_three, pool_pos[:, None, None], axis=1)[:, 0]
    normed_hf, norm_final, inv_final = masked_norm(
        pooled, gain_final.astype(f32), bias_final.astype(f32), col_keep, width_real
    )
    head_low = normed_hf.astype(bf16)
    projected = jnp.dot(head_low, w_embed, preferred_element_type=f32)
    inv_norm = lax.rsqrt(jnp.sum(projected * projected, axis=-1, keepdims=True) + NORM_EPS)
    embed_low = (projected * inv_norm).astype(bf16)
    own_all = lax.all_gather(embed_low, "dp", axis=0, tiled=True)
    others = swapped(own_all, "tower", 0)
    logit_mult = jnp.exp(logit_scale[0])
    similar = contract_cols(embed_low, others)
    logits = logit_mult * similar
    logit_top = jnp.max(logits, axis=-1, keepdims=True)
    logit_total = logit_top + jnp.log(jnp.sum(jnp.exp(logits - logit_top), axis=-1, keepdims=True))
    label_col = dp_index * samples + lax.broadcasted_iota(jnp.int32, (samples, 1), 0)
    label_hot = (lax.broadcasted_iota(jnp.int32, (samples, sample_total), 1) == label_col).astype(
        f32
    )
    diag_logit = jnp.sum(label_hot * logits, axis=-1, keepdims=True)
    loss_part = jnp.sum(logit_total - diag_logit) / (2.0 * sample_total)
    grad_logits = (jnp.exp(logits - logit_total) - label_hot) * 0.5
    scale_part = logit_mult * jnp.sum(grad_logits * similar)
    grad_sims = (logit_mult * grad_logits).astype(bf16)
    grad_own = jnp.dot(grad_sims, others, preferred_element_type=f32)
    grad_others = contract_rows(grad_sims, embed_low)
    sent_back = swapped(grad_others, "tower", 0)
    returned = lax.psum_scatter(sent_back, "dp", scatter_dimension=0, tiled=True)
    totals = lax.psum((loss_part, scale_part), ("tower", "dp"))
    grad_embed = grad_own + returned
    again = (
        lax.all_gather(ln1_gain[0], "dp", axis=0, tiled=True),
        lax.all_gather(qkv_weight[0], "dp", axis=0, tiled=True),
        lax.all_gather(out_weight[0], "dp", axis=0, tiled=True),
        lax.all_gather(ln2_gain[0], "dp", axis=0, tiled=True),
        lax.all_gather(fc_weight[0], "dp", axis=0, tiled=True),
        lax.all_gather(down_weight[0], "dp", axis=0, tiled=True),
        lax.all_gather(final_gain[0], "dp", axis=0, tiled=True),
        lax.all_gather(embed_weight[0], "dp", axis=0, tiled=True),
    )
    (
        back_gain_one,
        back_qkv,
        back_out,
        back_gain_two,
        back_fc,
        back_down,
        back_gain_final,
        back_embed,
    ) = again
    cross_term = jnp.sum(grad_embed * projected, axis=-1, keepdims=True)
    grad_proj = inv_norm * grad_embed - projected * inv_norm * inv_norm * inv_norm * cross_term
    grad_proj_low = grad_proj.astype(bf16)
    grad_head = contract_cols(grad_proj_low, back_embed)
    grad_pooled, d_gain_final, d_bias_final = masked_norm_back(
        grad_head, back_gain_final.astype(f32), norm_final, inv_final, col_keep, width_real
    )
    grad_rows = (pool_hot[:, :, None] * grad_pooled[:, None, :]).reshape(flat_rows, width_all)
    grad_branch_low = grad_rows.astype(bf16)
    d_down_b = column_sum(grad_branch_low)
    grad_act = contract_cols(grad_branch_low, back_down)
    grad_pre_low = (
        grad_act * (gate_sig + GELU_K * hidden_pre * gate_sig * (1.0 - gate_sig))
    ).astype(bf16)
    d_fc_b = column_sum(grad_pre_low)
    grad_norm_two = contract_cols(grad_pre_low, back_fc)
    grad_mid_norm, d_gain_two, d_bias_two = masked_norm_back(
        grad_norm_two, back_gain_two.astype(f32), norm_two, inv_two, col_keep, width_real
    )
    grad_middle = grad_rows + grad_mid_norm
    grad_attn_low = grad_middle.astype(bf16)
    d_out_b = column_sum(grad_attn_low)
    grad_mix_low = (
        contract_cols(grad_attn_low, back_out)
        .astype(bf16)
        .reshape(samples, seq_rows, head_count, HD)
    )
    probs_again = jnp.exp(masked_scores() - log_total)
    probs_low = probs_again.astype(bf16)
    grad_value = jnp.einsum("shqk,sqhd->skhd", probs_low, grad_mix_low, preferred_element_type=f32)
    grad_probs = jnp.einsum("sqhd,skhd->shqk", grad_mix_low, value_all, preferred_element_type=f32)
    grad_scores = probs_again * (
        grad_probs - jnp.sum(probs_again * grad_probs, axis=-1, keepdims=True)
    )
    grad_scores_low = grad_scores.astype(bf16)
    grad_query = (
        jnp.einsum("shqk,skhd->sqhd", grad_scores_low, key_all, preferred_element_type=f32)
        * score_mult
    )
    grad_key = (
        jnp.einsum("shqk,sqhd->skhd", grad_scores_low, query_all, preferred_element_type=f32)
        * score_mult
    )
    grad_qkv_low = (
        jnp.stack([grad_query, grad_key, grad_value], axis=2)
        .astype(bf16)
        .reshape(flat_rows, 3 * width_all)
    )
    d_qkv_w = contract_rows(normed_one, grad_qkv_low).reshape(width_all, 3, width_all)
    qkv_sums = column_sum(grad_qkv_low).reshape(3, width_all)
    d_qv_b = jnp.stack([qkv_sums[0], qkv_sums[2]])
    grad_norm_one = contract_cols(grad_qkv_low, back_qkv.reshape(width_all, 3 * width_all))
    grad_in_norm, d_gain_one, d_bias_one = masked_norm_back(
        grad_norm_one, back_gain_one.astype(f32), norm_one, inv_one, col_keep, width_real
    )
    tokens_grad = (grad_middle + grad_in_norm).reshape(1, samples, seq_rows, width_all)
    d_embed_w = contract_rows(head_low, grad_proj_low)
    d_down_w = contract_rows(act_low, grad_branch_low)
    d_fc_w = contract_rows(normed_two, grad_pre_low)
    d_out_w = contract_rows(head_mix_low, grad_attn_low)
    shares = (
        lax.psum_scatter(d_gain_one, "dp", scatter_dimension=0, tiled=True),
        lax.psum_scatter(d_bias_one, "dp", scatter_dimension=0, tiled=True),
        lax.psum_scatter(d_qkv_w, "dp", scatter_dimension=0, tiled=True),
        lax.psum_scatter(d_qv_b, "dp", scatter_dimension=1, tiled=True),
        lax.psum_scatter(d_out_w, "dp", scatter_dimension=0, tiled=True),
        lax.psum_scatter(d_out_b, "dp", scatter_dimension=0, tiled=True),
        lax.psum_scatter(d_gain_two, "dp", scatter_dimension=0, tiled=True),
        lax.psum_scatter(d_bias_two, "dp", scatter_dimension=0, tiled=True),
        lax.psum_scatter(d_fc_w, "dp", scatter_dimension=0, tiled=True),
        lax.psum_scatter(d_fc_b, "dp", scatter_dimension=0, tiled=True),
        lax.psum_scatter(d_down_w, "dp", scatter_dimension=0, tiled=True),
        lax.psum_scatter(d_down_b, "dp", scatter_dimension=0, tiled=True),
        lax.psum_scatter(d_gain_final, "dp", scatter_dimension=0, tiled=True),
        lax.psum_scatter(d_bias_final, "dp", scatter_dimension=0, tiled=True),
        lax.psum_scatter(d_embed_w, "dp", scatter_dimension=0, tiled=True),
    )
    results = list(shares)
    outputs = [item[None] for item in results]
    loss = totals[0].reshape(1)
    logit_scale_grad = totals[1].reshape(1)
    return (
        block_out,
        tokens_grad,
        loss,
        outputs[0],
        outputs[1],
        outputs[2],
        outputs[3],
        outputs[4],
        outputs[5],
        outputs[6],
        outputs[7],
        outputs[8],
        outputs[9],
        outputs[10],
        outputs[11],
        outputs[12],
        outputs[13],
        outputs[14],
        logit_scale_grad,
    )


def solution(mesh):
    return jax.shard_map(
        body,
        mesh=mesh,
        in_specs=(
            P("tower", "dp", None, None),
            P("dp"),
            P("tower", "dp"),
            P("tower", "dp"),
            P("tower", "dp", None, None),
            P("tower", None, "dp"),
            P("tower", "dp", None),
            P("tower", "dp"),
            P("tower", "dp"),
            P("tower", "dp"),
            P("tower", "dp", None),
            P("tower", "dp"),
            P("tower", "dp", None),
            P("tower", "dp"),
            P("tower", "dp"),
            P("tower", "dp"),
            P("tower", "dp", None),
            P(),
        ),
        out_specs=(
            P("tower", "dp", None, None),
            P("tower", "dp", None, None),
            P(),
            P("tower", "dp"),
            P("tower", "dp"),
            P("tower", "dp", None, None),
            P("tower", None, "dp"),
            P("tower", "dp", None),
            P("tower", "dp"),
            P("tower", "dp"),
            P("tower", "dp"),
            P("tower", "dp", None),
            P("tower", "dp"),
            P("tower", "dp", None),
            P("tower", "dp"),
            P("tower", "dp"),
            P("tower", "dp"),
            P("tower", "dp", None),
            P(),
        ),
        check_vma=False,
    )
```

profile of v0, /device:TPU:0, one launch (start us, length us, event | category | flops | bytes accessed | tf_op | source)
XLA Modules:
  0.0 893.0 jit_solution(10914504779432311410)
XLA Ops:
  17.1 63.5 %all-reduce.20 = (bf16[768]{0:T(1024)(128)(2,1)S(1)}, bf16[768]{0:T(1024)(128)(2,1)S(1)}, bf16[768]{0:T(1024)(128)(2,1)S(1)}, bf16[768]{0:T(1024)(128)(2,1)S(1)}...) all-reduce(bf16[768]{0:T(1024)(128)(2,1)S(1)} %dynamic-update-slice, ...), channel_id=3, replica_groups=mesh['tower'=2,'dp'=16] {'dp'}, use_global_device_ids=true, to_apply=%add.1 | all-reduce | flops 9216 | bytes 36864
  87.5 18.4 %all-gather.3 = bf16[1,2,768]{1,0,2:T(2,128)(2,1)S(1)} all-gather(bf16[1,2,48]{1,0,2:T(2,128)(2,1)S(1)} %copy.125), channel_id=5, replica_groups=mesh['tower'=2,'dp'=16] {'dp'}, dimensions={2}, use_global_device_ids=true | all-gather | bytes 3264 | tf_op jit(solution)/shard_map/all_gather | solution.py:107
  106.6 4.7 fusion.37
  113.2 25.5 %all-gather.14 = bf16[1,768,512]{2,1,0:T(8,128)(2,1)} all-gather(bf16[1,48,512]{2,1,0:T(8,128)(2,1)S(1)} %copy-done.29), channel_id=16, replica_groups=mesh['tower'=2,'dp'=16] {'dp'}, dimensions={1}, use_global_device_ids=true | all-gather | bytes 835584 | tf_op jit(solution)/shard_map/all_gather | solution.py:118
  138.7 4.8 copy.124
  143.5 5.9 add_convert_fusion
  149.4 9.7 %reshape.511 = bf16[8,77,3,12,64]{4,3,2,1,0:T(8,128)(2,1)} reshape(bf16[616,2304]{1,0:T(8,128)(2,1)} %add_convert_fusion) | data formatting | bytes 5677056 | tf_op jit(solution)/shard_map/reshape | solution.py:149
  159.1 5.4 fusion.56
  164.5 4.0 copy.156
  168.5 3.9 copy.155
  172.4 5.1 copy.154
  183.3 2.0 reshape.383
  185.3 3.3 multiply_reduce_fusion.6
  189.1 8.2 fusion.5
  197.3 13.7 %all-gather.26.cloned.1.call-done = bf16[1,3072,768]{2,1,0:T(8,128)(2,1)} async-done(((bf16[1,192,768]{2,1,0:T(8,128)(2,1)}), bf16[1,3072,768]{2,1,0:T(8,128)(2,1)}) %all-gather.26.cloned.1.call-update) | async-done | bytes 4718608 | tf_op jit(solution)/shard_map/all_gather | solution.py:114
  211.0 10.2 %fusion.60 = (bf16[616,768]{1,0:T(8,128)(2,1)}, f32[616,768]{1,0:T(8,128)}) fusion(f32[616,768]{1,0:T(8,128)S(1)} %get-tuple-element.166, f32[768]{0:T(1024)S(1)} %copy-done.56, bf16[1,3072,768]{2,1,0:T(8,128)(2,1)} %all-gather.26.cloned.1.call-done, f32[616,3072]{1,0:T(8,128)} %fusion.5, f32[3072]{0:T(1024)S(1)} %copy-done.48, f32[616]{0:T(1024)S(1)} %copy-done.57), kind=kOutput, calls=%fused_computation.149 | convolution fusion | flops 2921791488 | bytes 17036704 | tf_op jit(solution)/shard_map/dot_general | solution.py:178
  221.2 3.1 reshape.385
  224.3 3.9 copy.132
  231.6 20.7 %all_gather.71 = bf16[128,512]{1,0:T(8,128)(2,1)} all-gather(bf16[8,512]{1,0:T(8,128)(2,1)S(1)} %multiply_convert_fusion.5), channel_id=1, replica_groups=mesh['tower'=2,'dp'=16] {'dp'}, dimensions={0}, use_global_device_ids=true | all-gather | bytes 139264 | tf_op jit(solution)/shard_map/all_gather | solution.py:190
  254.4 3.9 collective-permute-done
  261.5 6.4 collective-permute-done.1
  270.9 49.7 %reduce-scatter.10.cloned.1.call-done = f32[8,512]{1,0:T(8,128)} async-done(((f32[128,512]{1,0:T(8,128)}), f32[8,512]{1,0:T(8,128)}) %reduce-scatter.10.cloned.1.call-update) | async-done | bytes 16400 | tf_op jit(solution)/shard_map/reduce_scatter | solution.py:209
  322.7 2.1 multiply_reduce_fusion.11
  327.7 3.0 mul.407
  330.7 9.5 %convert_reduce_fusion.1 = (f32[3072]{0:T(1024)}, bf16[616,3072]{1,0:T(8,128)(2,1)S(1)}) fusion(f32[616,3072]{1,0:T(8,128)} %fusion.5, f32[3072]{0:T(1024)} %convert_element_type.252, bf16[1,3072,768]{2,1,0:T(8,128)(2,1)} %all-gather.26.cloned.1.call-done, f32[616,768]{1,0:T(8,128)} %mul.407, f32[616]{0:T(1024)} %reshape.394), kind=kOutput, calls=%fused_computation.3 | convolution fusion | flops 2932196352 | bytes 17992096 | tf_op jit(solution)/shard_map/dot_general | solution.py:50
  340.3 8.0 multiply_reduce_fusion.1
  348.3 3.0 convert_reduce_fusion.3
  351.2 1.9 convolution_convert_fusion
  353.1 4.1 reshape.512
  357.2 4.7 copy.134
  362.0 3.9 fusion.13
  371.2 3.1 convert_reduce_fusion
  375.6 1.7 fusion.49
  377.4 2.6 fusion.45
  382.4 13.8 %copy.139 = bf16[8,77,3,12,64]{1,0,4,3,2:T(8,128)(2,1)} copy(bf16[8,77,3,12,64]{1,4,3,0,2:T(8,128)(2,1)} %get-tuple-element.151) | data formatting | bytes 5677056 | tf_op jit(solution)/shard_map/convert_element_type | solution.py:277
  396.1 8.1 convert_element_type.224
  404.2 6.8 fusion.61
  411.2 10.5 %fusion.39 = f32[768,3072]{1,0:T(8,128)} fusion(bf16[616,3072]{1,0:T(8,128)(2,1)} %copy-done.14, f32[768]{0:T(1024)S(1)} %convert_element_type.251, f32[768]{0:T(1024)S(1)} %convert_element_type.250, f32[616,768]{1,0:T(8,128)} %copy-done.2, f32[616]{0:T(1024)S(1)} %add_rsqrt_fusion, f32[616]{0:T(1024)S(1)} %broadcast_divide_fusion.4, f32[768]{0:T(1024)S(1)} %fusion.43), kind=kOutput, calls=%fused_computation.76 | convolution fusion | flops 2909491200 | bytes 15128384 | tf_op jit(solution)/shard_map/dot_general | solution.py:44
  422.3 12.2 %fusion.53 = f32[3072,768]{1,0:T(8,128)} fusion(f32[616,768]{1,0:T(8,128)} %mul.407, f32[616]{0:T(1024)S(1)} %copy-done.44, f32[616,3072]{1,0:T(8,128)} %fusion.5, f32[3072]{0:T(1024)S(1)} %copy-done.49), kind=kOutput, calls=%fused_computation.144 | convolution fusion | flops 2920845312 | bytes 18913696 | tf_op jit(solution)/shard_map/dot_general | solution.py:44
  442.0 41.8 %all-reduce.18 = (f32[1]{0:T(128)}, f32[1]{0:T(128)}) all-reduce(f32[1]{0:T(128)} %bitcast.29, f32[1]{0:T(128)} %bitcast.47), channel_id=1, replica_groups=mesh['tower'=2,'dp'=16] {'tower','dp'}, use_global_device_ids=true, to_apply=%region_22.23 | all-reduce | flops 2 | bytes 16 | tf_op jit(solution)/shard_map/psum | solution.py:210
  483.8 6.6 multiply_reduce_fusion.2
  490.5 2.0 multiply_add_fusion
  492.5 1.8 reshape.387
  494.3 2.3 copy.142
  497.0 58.9 %all-reduce.19 = (f32[768]{0:T(1024)S(1)}, f32[768]{0:T(1024)S(1)}, f32[768]{0:T(1024)S(1)}, f32[768]{0:T(1024)S(1)}, f32[768]{0:T(1024)S(1)}, /*index=5*/f32[30...) all-reduce(f32[768]{0:T(1024)S(1)} %get-tuple-element.116, ...), channel_id=18, replica_groups=mesh['tower'=2,'dp'=16] {'dp'}, use_global_device_ids=true, to_apply=%region_24.25.clone | all-reduce | flops 9216 | bytes 73728
  560.2 94.2 %reduce-scatter.12.cloned.1.call-done = f32[48,3,768]{2,0,1:T(8,128)} async-done(((f32[768,3,768]{2,0,1:T(8,128)}), f32[48,3,768]{2,0,1:T(8,128)}) %reduce-scatter.12.cloned.1.call-update) | async-done | bytes 442384 | tf_op jit(solution)/shard_map/reduce_scatter | solution.py:295
  654.4 115.4 %reduce-scatter.16.cloned.1.call-done = f32[48,3072]{1,0:T(8,128)} async-done(((f32[768,3072]{1,0:T(8,128)}), f32[48,3072]{1,0:T(8,128)}) %reduce-scatter.16.cloned.1.call-update) | async-done | bytes 589840 | tf_op jit(solution)/shard_map/reduce_scatter | solution.py:301
  769.8 116.4 %reduce-scatter.18.cloned.1.call-done = f32[192,768]{1,0:T(8,128)} async-done(((f32[3072,768]{1,0:T(8,128)}), f32[192,768]{1,0:T(8,128)}) %reduce-scatter.18.cloned.1.call-update) | async-done | bytes 589840 | tf_op jit(solution)/shard_map/reduce_scatter | solution.py:303
  (299 shorter events, 58.9 us)
Async XLA Ops:
  7.2 131.5 %all-gather.20.cloned.1.call-start = ((), (), s32[]{:S(2)}) async-start(), calls=%async_computation.13 | async-start | bytes 3760128 | tf_op jit(solution)/shard_map/all_gather | solution.py:106
  7.9 177.4 %all-gather.22.cloned.1.call-start = ((), (), s32[]{:S(2)}) async-start(), calls=%async_computation.14 | async-start | bytes 1253376 | tf_op jit(solution)/shard_map/all_gather | solution.py:108
  8.7 180.4 %all-gather.24.cloned.1.call-start = ((), (), s32[]{:S(2)}) async-start(), calls=%async_computation.15 | async-start | bytes 5013504 | tf_op jit(solution)/shard_map/all_gather | solution.py:112
  9.4 201.6 %all-gather.26.cloned.1.call-start = ((), (), s32[]{:S(2)}) async-start(), calls=%async_computation.16 | async-start | bytes 5013504 | tf_op jit(solution)/shard_map/all_gather | solution.py:114
  10.0 310.7 %reduce-scatter.10.cloned.1.call-start = ((), (), s32[]{:S(2)}) async-start(), calls=%async_computation.7 | async-start | bytes 278528 | tf_op jit(solution)/shard_map/reduce_scatter | solution.py:209
  11.5 4.6 copy-start.76
  11.5 4.9 copy-start.67
  11.5 4.9 copy-start.77
  11.5 5.1 copy-start.78
  11.6 69.6 %copy-start.3 = (bf16[1,8,77,768]{3,1,2,0:T(8,128)(2,1)S(1)}, bf16[1,8,77,768]{3,1,2,0:T(8,128)(2,1)}, u32[]{:S(2)}) copy-start(bf16[1,8,77,768]{3,1,2,0:T(8,128)(2,1)} %param.18) | copy-start | bytes 2838532
  83.6 55.1 %copy-start.7 = (bf16[1,8,77,768]{3,2,1,0:T(8,128)(2,1)}, bf16[1,8,77,768]{3,2,1,0:T(8,128)(2,1)S(1)}, u32[]{:S(2)}) copy-start(bf16[1,8,77,768]{3,2,1,0:T(8,128)(2,1)S(1)} %copy.123) | copy-start | bytes 2838532
  83.6 29.6 %copy-start.29 = (bf16[1,48,512]{2,1,0:T(8,128)(2,1)S(1)}, bf16[1,48,512]{2,1,0:T(8,128)(2,1)}, u32[]{:S(2)}) copy-start(bf16[1,48,512]{2,1,0:T(8,128)(2,1)} %param.34) | copy-start | bytes 147460
  106.5 32.2 %copy-start.66 = (s32[8]{0:T(128)}, s32[8]{0:T(128)S(1)}, u32[]{:S(2)}) copy-start(s32[8]{0:T(128)S(1)} %get-tuple-element.155) | copy-start | bytes 100
  143.5 5.9 copy-start.15
  172.4 5.1 copy-start.4
  172.4 5.1 copy-start.20
  188.6 151.7 %copy-start.2 = (f32[616,768]{1,0:T(8,128)}, f32[616,768]{1,0:T(8,128)S(1)}, u32[]{:S(2)}) copy-start(f32[616,768]{1,0:T(8,128)S(1)} %get-tuple-element.166) | copy-start | bytes 5677060
  189.0 21.9 %copy-start.48 = (f32[3072]{0:T(1024)S(1)}, f32[3072]{0:T(1024)}, u32[]{:S(2)}) copy-start(f32[3072]{0:T(1024)} %convert_element_type.252) | copy-start | bytes 36868
  189.1 21.9 %copy-start.56 = (f32[768]{0:T(1024)S(1)}, f32[768]{0:T(1024)}, u32[]{:S(2)}) copy-start(f32[768]{0:T(1024)} %convert_element_type.253) | copy-start | bytes 9220
  189.1 21.9 %copy-start.57 = (f32[616]{0:T(1024)S(1)}, f32[616]{0:T(1024)}, u32[]{:S(2)}) copy-start(f32[616]{0:T(1024)} %reshape.390) | copy-start | bytes 7396
  224.3 5.3 copy-start.39
  224.3 5.7 copy-start.41
  229.5 39.2 %copy-start.17 = (f32[8,768]{1,0:T(8,128)}, f32[8,768]{1,0:T(8,128)S(1)}, u32[]{:S(2)}) copy-start(f32[8,768]{1,0:T(8,128)S(1)} %gather_fusion) | copy-start | bytes 73732
  230.0 38.8 %copy-start.53 = (f32[8]{0:T(128)}, f32[8]{0:T(128)S(1)}, u32[]{:S(2)}) copy-start(f32[8]{0:T(128)S(1)} %add_rsqrt_fusion.3) | copy-start | bytes 100
  231.5 23.0 %copy-start.28 = (f32[8,512]{1,0:T(8,128)}, f32[8,512]{1,0:T(8,128)S(1)}, u32[]{:S(2)}) copy-start(f32[8,512]{1,0:T(8,128)S(1)} %get-tuple-element.170) | copy-start | bytes 49156
  231.5 37.2 %copy-start.60 = (f32[8]{0:T(128)}, f32[8]{0:T(128)S(1)}, u32[]{:S(2)}) copy-start(f32[8]{0:T(128)S(1)} %add_rsqrt_fusion.2) | copy-start | bytes 100
  252.3 6.1 collective-permute-start
  254.4 14.3 %copy-start.61 = (s32[8]{0:T(128)}, s32[8]{0:T(128)S(1)}, u32[]{:S(2)}) copy-start(s32[8]{0:T(128)S(1)} %iota_add_fusion) | copy-start | bytes 100
  259.5 9.3 %copy-start.26 = (f32[8,128]{1,0:T(8,128)}, f32[8,128]{1,0:T(8,128)S(1)}, u32[]{:S(2)}) copy-start(f32[8,128]{1,0:T(8,128)S(1)} %get-tuple-element.172) | copy-start | bytes 12292
  259.7 9.1 %copy-start.63 = (f32[8]{0:T(128)}, f32[8]{0:T(128)S(1)}, u32[]{:S(2)}) copy-start(f32[8]{0:T(128)S(1)} %log_add_fusion.1) | copy-start | bytes 100
  260.0 7.9 collective-permute-start.1
  268.0 290.9 %reduce-scatter.22.cloned.1.call-start = ((), (), s32[]{:S(2)}) async-start(), calls=%async_computation.17 | async-start | bytes 417792
  340.2 8.0 copy-start.14
  340.2 8.0 copy-start.10
  340.3 8.0 copy-start.43
  362.0 4.7 copy-start.12
  371.1 4.4 copy-start.18
  371.2 4.4 copy-start.25
  371.2 4.4 copy-start.40
  371.2 4.4 copy-start.42
  375.5 184.7 %reduce-scatter.20.cloned.1.call-start = ((), (), s32[]{:S(2)}) async-start(), calls=%async_computation.12 | async-start | bytes 1671168 | tf_op jit(solution)/shard_map/reduce_scatter | solution.py:307
  377.3 182.9 %reduce-scatter.14.cloned.1.call-start = ((), (), s32[]{:S(2)}) async-start(), calls=%async_computation.9 | async-start | bytes 2506752 | tf_op jit(solution)/shard_map/reduce_scatter | solution.py:297
  380.0 274.5 %reduce-scatter.12.cloned.1.call-start = ((), (), s32[]{:S(2)}) async-start(), calls=%async_computation.8 | async-start | bytes 7520256 | tf_op jit(solution)/shard_map/reduce_scatter | solution.py:295
  396.1 8.1 copy-start.16
  411.1 358.7 %reduce-scatter.16.cloned.1.call-start = ((), (), s32[]{:S(2)}) async-start(), calls=%async_computation.10 | async-start | bytes 10027008 | tf_op jit(solution)/shard_map/reduce_scatter | solution.py:301
  421.6 464.6 %reduce-scatter.18.cloned.1.call-start = ((), (), s32[]{:S(2)}) async-start(), calls=%async_computation.11 | async-start | bytes 10027008 | tf_op jit(solution)/shard_map/reduce_scatter | solution.py:303
  436.7 47.2 %copy-start.31 = (f32[768]{0:T(1024)S(1)}, f32[768]{0:T(1024)}, u32[]{:S(2)}) copy-start(f32[768]{0:T(1024)} %copy-done.30) | copy-start | bytes 9220
  483.8 6.7 copy-start.9
  (44 other events, 103.4 us)
Sparse Core Ops, SparseCore 0:
  10.3 50.0 all-gather.19
  62.7 38.0 all-gather.21
  103.1 53.8 all-gather.23
  159.1 51.8 all-gather.25
  268.1 52.5 reduce-scatter.9
  375.6 54.6 reduce-scatter.21
  435.0 58.5 reduce-scatter.19
  497.9 62.1 reduce-scatter.13
  565.3 89.1 reduce-scatter.11
  658.9 110.8 reduce-scatter.15
  775.0 111.1 reduce-scatter.17
where the time goes:
time: 902 us; the launch traced here: 893 us
  waiting for transfers between devices  402 us (45%)
  blocking collectives  229 us (25%)
  local copies, waits for them, and re-layouts  109 us (12%)
  matrix products  102 us (11%)
  other arithmetic  27 us (3%)
  between operations  19.8 us (2%)
    unnamed x2, blocking collectives  122 us
    reduce_scatter x1, waiting for transfers between devices, body(): lax.psum_scatter(d_down_w, 'dp', scatter_dimension=0, tiled=True)  116 us
    reduce_scatter x1, waiting for transfers between devices, body(): lax.psum_scatter(d_fc_w, 'dp', scatter_dimension=0, tiled=True)  115 us
    reduce_scatter x1, waiting for transfers between devices, body(): lax.psum_scatter(d_qkv_w, 'dp', scatter_dimension=0, tiled=True)  94.2 us
    reduce_scatter x1, waiting for transfers between devices, body(): lax.psum_scatter(sent_back, 'dp', scatter_dimension=0, tiled=True)  49.7 us
    psum x1, blocking collectives, body(): totals = lax.psum((loss_part, scale_part), ('tower', 'dp'))  41.8 us
    dot_general x6, matrix products, contract_rows(): lax.dot_general(left_op, right_op, (((0,), (0,)), ((), ())), preferred_el...  34 us
    dot_general x6, matrix products, contract_cols(): lax.dot_general(left_op, right_op, (((1,), (1,)), ((), ())), preferred_el...  29.3 us
  transfers between devices with their start and end apart: 13, of which 7 were waited for; matrix products, arithmetic and copies ran while one was open for 18% of the time, Pallas kernels for 0%

commit v1 on v0

--- a/solution.py
+++ b/solution.py
@@ -187,7 +187,12 @@
     projected = jnp.dot(head_low, w_embed, preferred_element_type=f32)
     inv_norm = lax.rsqrt(jnp.sum(projected * projected, axis=-1, keepdims=True) + NORM_EPS)
     embed_low = (projected * inv_norm).astype(bf16)
-    own_all = lax.all_gather(embed_low, "dp", axis=0, tiled=True)
+    ring = [embed_low]
+    for hop in range(15):
+        ring.append(lax.ppermute(ring[-1], "dp", [(dev, (dev + 1) % 16) for dev in range(16)]))
+    own_all = jnp.roll(
+        jnp.concatenate(ring[::-1], axis=0), (lax.axis_index("dp") + 1) * ring[0].shape[0], axis=0
+    )
     others = swapped(own_all, "tower", 0)
     logit_mult = jnp.exp(logit_scale[0])
     similar = contract_cols(embed_low, others)

time: 902 us -> 996 us (1.10)
  waiting for transfers between devices: 402 us -> 488 us
  local copies, waits for them, and re-layouts: 109 us -> 134 us
  blocking collectives: 229 us -> 208 us
    ppermute x0 -> x15, waiting for transfers between devices: none -> 86.7 us  [body(): lax.ppermute(ring[-1], 'dp', [(dev, (dev + 1) % 16) for dev in range(16)])]
    unnamed x187 -> x239, local copies, waits for them, and re-layouts: 28.9 us -> 54 us
    all_gather x1 -> x0, blocking collectives: 20.7 us -> none  [body(): own_all = lax.all_gather(embed_low, 'dp', axis=0, tiled=True)]
  transfers between devices with their start and end apart: 13 -> 28, of which waited for: 7 -> 22; matrix products, arithmetic and copies ran while one was open for 18% -> 16% of each run, Pallas kernels for 0% -> 0%
where the time goes in v1:
time: 996 us; the launch traced here: 986 us
  waiting for transfers between devices  488 us (49%)
  blocking collectives  208 us (21%)
  local copies, waits for them, and re-layouts  134 us (13%)
  matrix products  102 us (10%)
  other arithmetic  28.4 us (3%)
  between operations  19.8 us (2%)
    unnamed x2, blocking collectives  122 us
    reduce_scatter x1, waiting for transfers between devices, body(): lax.psum_scatter(d_down_w, 'dp', scatter_dimension=0, tiled=True)  116 us
    reduce_scatter x1, waiting for transfers between devices, body(): lax.psum_scatter(d_fc_w, 'dp', scatter_dimension=0, tiled=True)  115 us
    reduce_scatter x1, waiting for transfers between devices, body(): lax.psum_scatter(d_qkv_w, 'dp', scatter_dimension=0, tiled=True)  94.1 us
    ppermute x15, waiting for transfers between devices, body(): lax.ppermute(ring[-1], 'dp', [(dev, (dev + 1) % 16) for dev in range(16)])  86.7 us
    unnamed x239, local copies, waits for them, and re-layouts  54 us
    reduce_scatter x1, waiting for transfers between devices, body(): lax.psum_scatter(sent_back, 'dp', scatter_dimension=0, tiled=True)  49.8 us
    psum x1, blocking collectives, body(): totals = lax.psum((loss_part, scale_part), ('tower', 'dp'))  41.8 us
  transfers between devices with their start and end apart: 28, of which 22 were waited for; matrix products, arithmetic and copies ran while one was open for 16% of the time, Pallas kernels for 0%

profile of v1, /device:TPU:0, one launch (start us, length us, event | category | flops | bytes accessed | tf_op | source)
XLA Modules:
  0.0 985.6 jit_solution(15370951535657338658)
XLA Ops:
  17.1 63.5 %all-reduce.20 = (bf16[768]{0:T(1024)(128)(2,1)S(1)}, bf16[768]{0:T(1024)(128)(2,1)S(1)}, bf16[768]{0:T(1024)(128)(2,1)S(1)}, bf16[768]{0:T(1024)(128)(2,1)S(1)}...) all-reduce(bf16[768]{0:T(1024)(128)(2,1)S(1)} %dynamic-update-slice, ...), channel_id=3, replica_groups=mesh['tower'=2,'dp'=16] {'dp'}, use_global_device_ids=true, to_apply=%add.1 | all-reduce | flops 9216 | bytes 36864
  87.5 18.5 %all-gather.3 = bf16[1,2,768]{1,0,2:T(2,128)(2,1)S(1)} all-gather(bf16[1,2,48]{1,0,2:T(2,128)(2,1)S(1)} %copy.125), channel_id=5, replica_groups=mesh['tower'=2,'dp'=16] {'dp'}, dimensions={2}, use_global_device_ids=true | all-gather | bytes 3264 | tf_op jit(solution)/shard_map/all_gather | solution.py:107
  106.6 4.7 fusion.37
  113.2 25.5 %all-gather.14 = bf16[1,768,512]{2,1,0:T(8,128)(2,1)} all-gather(bf16[1,48,512]{2,1,0:T(8,128)(2,1)S(1)} %copy-done.29), channel_id=16, replica_groups=mesh['tower'=2,'dp'=16] {'dp'}, dimensions={1}, use_global_device_ids=true | all-gather | bytes 835584 | tf_op jit(solution)/shard_map/all_gather | solution.py:118
  138.7 4.8 copy.124
  143.5 5.9 add_convert_fusion
  149.4 9.7 reshape.511
  159.1 5.5 fusion.56
  164.5 4.0 copy.156
  168.5 3.9 copy.155
  172.5 5.1 copy.154
  189.1 8.2 fusion.5
  197.2 13.7 %all-gather.26.cloned.1.call-done = bf16[1,3072,768]{2,1,0:T(8,128)(2,1)} async-done(((bf16[1,192,768]{2,1,0:T(8,128)(2,1)}), bf16[1,3072,768]{2,1,0:T(8,128)(2,1)}) %all-gather.26.cloned.1.call-update) | async-done | bytes 4718608 | tf_op jit(solution)/shard_map/all_gather | solution.py:114
  211.0 10.2 %fusion.60 = (bf16[616,768]{1,0:T(8,128)(2,1)}, f32[616,768]{1,0:T(8,128)}) fusion(f32[616,768]{1,0:T(8,128)S(1)} %get-tuple-element.166, f32[768]{0:T(1024)S(1)} %copy-done.68, bf16[1,3072,768]{2,1,0:T(8,128)(2,1)} %all-gather.26.cloned.1.call-done, f32[616,3072]{1,0:T(8,128)} %fusion.5, f32[3072]{0:T(1024)S(1)} %copy-done.59, f32[616]{0:T(1024)S(1)} %copy-done.69), kind=kOutput, calls=%fused_computation.182 | convolution fusion | flops 2921791488 | bytes 17036704 | tf_op jit(solution)/shard_map/dot_general | solution.py:178
  232.3 5.5 collective-permute-done
  237.8 5.8 collective-permute-done.1
  243.5 5.8 collective-permute-done.2
  249.9 5.8 collective-permute-done.3
  256.3 5.8 collective-permute-done.4
  262.6 5.8 collective-permute-done.5
  269.0 5.8 collective-permute-done.6
  275.4 5.8 collective-permute-done.7
  281.8 5.8 collective-permute-done.8
  288.1 5.8 collective-permute-done.9
  294.5 5.8 collective-permute-done.10
  300.9 5.8 collective-permute-done.11
  307.2 5.8 collective-permute-done.12
  313.6 5.9 collective-permute-done.13
  319.5 6.1 collective-permute-done.14
  348.0 4.3 collective-permute-done.15
  355.6 5.0 collective-permute-done.16
  363.6 49.8 %reduce-scatter.10.cloned.1.call-done = f32[8,512]{1,0:T(8,128)} async-done(((f32[128,512]{1,0:T(8,128)}), f32[8,512]{1,0:T(8,128)}) %reduce-scatter.10.cloned.1.call-update) | async-done | bytes 16400 | tf_op jit(solution)/shard_map/reduce_scatter | solution.py:214
  423.5 9.5 convert_reduce_fusion.1
  433.0 8.0 multiply_reduce_fusion.1
  445.9 4.1 reshape.512
  449.9 4.7 copy.134
  454.7 3.9 fusion.13
  475.1 13.8 %copy.139 = bf16[8,77,3,12,64]{1,0,4,3,2:T(8,128)(2,1)} copy(bf16[8,77,3,12,64]{1,4,3,0,2:T(8,128)(2,1)} %get-tuple-element.151) | data formatting | bytes 5677056 | tf_op jit(solution)/shard_map/convert_element_type | solution.py:282
  488.9 8.1 convert_element_type.224
  497.0 6.9 fusion.61
  503.9 10.5 %fusion.39 = f32[768,3072]{1,0:T(8,128)} fusion(bf16[616,3072]{1,0:T(8,128)(2,1)} %copy-done.14, f32[768]{0:T(1024)S(1)} %convert_element_type.251, f32[768]{0:T(1024)S(1)} %convert_element_type.250, f32[616,768]{1,0:T(8,128)} %copy-done.2, f32[616]{0:T(1024)S(1)} %add_rsqrt_fusion, f32[616]{0:T(1024)S(1)} %broadcast_divide_fusion.4, f32[768]{0:T(1024)S(1)} %fusion.43), kind=kOutput, calls=%fused_computation.76 | convolution fusion | flops 2909491200 | bytes 15128384 | tf_op jit(solution)/shard_map/dot_general | solution.py:44
  515.1 12.1 %fusion.53 = f32[3072,768]{1,0:T(8,128)} fusion(f32[616,768]{1,0:T(8,128)} %mul.411, f32[616]{0:T(1024)S(1)} %copy-done.55, f32[616,3072]{1,0:T(8,128)} %fusion.5, f32[3072]{0:T(1024)S(1)} %copy-done.60), kind=kOutput, calls=%fused_computation.177 | convolution fusion | flops 2920845312 | bytes 18913696 | tf_op jit(solution)/shard_map/dot_general | solution.py:44
  534.7 41.8 %all-reduce.18 = (f32[1]{0:T(128)}, f32[1]{0:T(128)}) all-reduce(f32[1]{0:T(128)} %bitcast.29, f32[1]{0:T(128)} %bitcast.47), channel_id=1, replica_groups=mesh['tower'=2,'dp'=16] {'tower','dp'}, use_global_device_ids=true, to_apply=%region_22.23 | all-reduce | flops 2 | bytes 16 | tf_op jit(solution)/shard_map/psum | solution.py:215
  576.6 6.7 multiply_reduce_fusion.2
  589.7 59.0 %all-reduce.19 = (f32[768]{0:T(1024)S(1)}, f32[768]{0:T(1024)S(1)}, f32[768]{0:T(1024)S(1)}, f32[768]{0:T(1024)S(1)}, f32[768]{0:T(1024)S(1)}, /*index=5*/f32[30...) all-reduce(f32[768]{0:T(1024)S(1)} %get-tuple-element.116, ...), channel_id=18, replica_groups=mesh['tower'=2,'dp'=16] {'dp'}, use_global_device_ids=true, to_apply=%region_24.25.clone | all-reduce | flops 9216 | bytes 73728
  653.0 94.1 %reduce-scatter.12.cloned.1.call-done = f32[48,3,768]{2,0,1:T(8,128)} async-done(((f32[768,3,768]{2,0,1:T(8,128)}), f32[48,3,768]{2,0,1:T(8,128)}) %reduce-scatter.12.cloned.1.call-update) | async-done | bytes 442384 | tf_op jit(solution)/shard_map/reduce_scatter | solution.py:300
  747.1 115.4 %reduce-scatter.16.cloned.1.call-done = f32[48,3072]{1,0:T(8,128)} async-done(((f32[768,3072]{1,0:T(8,128)}), f32[48,3072]{1,0:T(8,128)}) %reduce-scatter.16.cloned.1.call-update) | async-done | bytes 589840 | tf_op jit(solution)/shard_map/reduce_scatter | solution.py:306
  862.5 116.4 %reduce-scatter.18.cloned.1.call-done = f32[192,768]{1,0:T(8,128)} async-done(((f32[3072,768]{1,0:T(8,128)}), f32[192,768]{1,0:T(8,128)}) %reduce-scatter.18.cloned.1.call-update) | async-done | bytes 589840 | tf_op jit(solution)/shard_map/reduce_scatter | solution.py:308
  (383 shorter events, 122.1 us)
Async XLA Ops:
  7.2 131.5 %all-gather.20.cloned.1.call-start = ((), (), s32[]{:S(2)}) async-start(), calls=%async_computation.13 | async-start | bytes 3760128 | tf_op jit(solution)/shard_map/all_gather | solution.py:106
  7.9 177.4 %all-gather.22.cloned.1.call-start = ((), (), s32[]{:S(2)}) async-start(), calls=%async_computation.14 | async-start | bytes 1253376 | tf_op jit(solution)/shard_map/all_gather | solution.py:108
  8.7 180.4 %all-gather.24.cloned.1.call-start = ((), (), s32[]{:S(2)}) async-start(), calls=%async_computation.15 | async-start | bytes 5013504 | tf_op jit(solution)/shard_map/all_gather | solution.py:112
  9.4 201.6 %all-gather.26.cloned.1.call-start = ((), (), s32[]{:S(2)}) async-start(), calls=%async_computation.16 | async-start | bytes 5013504 | tf_op jit(solution)/shard_map/all_gather | solution.py:114
  10.0 403.4 %reduce-scatter.10.cloned.1.call-start = ((), (), s32[]{:S(2)}) async-start(), calls=%async_computation.7 | async-start | bytes 278528 | tf_op jit(solution)/shard_map/reduce_scatter | solution.py:214
  11.6 69.6 %copy-start.3 = (bf16[1,8,77,768]{3,1,2,0:T(8,128)(2,1)S(1)}, bf16[1,8,77,768]{3,1,2,0:T(8,128)(2,1)}, u32[]{:S(2)}) copy-start(bf16[1,8,77,768]{3,1,2,0:T(8,128)(2,1)} %param.18) | copy-start | bytes 2838532
  83.6 55.1 %copy-start.7 = (bf16[1,8,77,768]{3,2,1,0:T(8,128)(2,1)}, bf16[1,8,77,768]{3,2,1,0:T(8,128)(2,1)S(1)}, u32[]{:S(2)}) copy-start(bf16[1,8,77,768]{3,2,1,0:T(8,128)(2,1)S(1)} %copy.123) | copy-start | bytes 2838532
  83.6 29.6 %copy-start.29 = (bf16[1,48,512]{2,1,0:T(8,128)(2,1)S(1)}, bf16[1,48,512]{2,1,0:T(8,128)(2,1)}, u32[]{:S(2)}) copy-start(bf16[1,48,512]{2,1,0:T(8,128)(2,1)} %param.34) | copy-start | bytes 147460
  106.5 32.2 %copy-start.77 = (s32[8]{0:T(128)}, s32[8]{0:T(128)S(1)}, u32[]{:S(2)}) copy-start(s32[8]{0:T(128)S(1)} %get-tuple-element.155) | copy-start | bytes 100
  143.5 5.9 copy-start.15
  188.5 244.4 %copy-start.2 = (f32[616,768]{1,0:T(8,128)}, f32[616,768]{1,0:T(8,128)S(1)}, u32[]{:S(2)}) copy-start(f32[616,768]{1,0:T(8,128)S(1)} %get-tuple-element.166) | copy-start | bytes 5677060
  189.0 22.0 %copy-start.59 = (f32[3072]{0:T(1024)S(1)}, f32[3072]{0:T(1024)}, u32[]{:S(2)}) copy-start(f32[3072]{0:T(1024)} %convert_element_type.252) | copy-start | bytes 36868
  189.0 22.0 %copy-start.68 = (f32[768]{0:T(1024)S(1)}, f32[768]{0:T(1024)}, u32[]{:S(2)}) copy-start(f32[768]{0:T(1024)} %convert_element_type.253) | copy-start | bytes 9220
  189.0 22.0 %copy-start.69 = (f32[616]{0:T(1024)S(1)}, f32[616]{0:T(1024)}, u32[]{:S(2)}) copy-start(f32[616]{0:T(1024)} %reshape.390) | copy-start | bytes 7396
  229.4 132.0 %copy-start.17 = (f32[8,768]{1,0:T(8,128)}, f32[8,768]{1,0:T(8,128)S(1)}, u32[]{:S(2)}) copy-start(f32[8,768]{1,0:T(8,128)S(1)} %gather_fusion) | copy-start | bytes 73732
  231.4 130.0 %copy-start.22 = (f32[8,512]{1,0:T(8,128)}, f32[8,512]{1,0:T(8,128)S(1)}, u32[]{:S(2)}) copy-start(f32[8,512]{1,0:T(8,128)S(1)} %get-tuple-element.170) | copy-start | bytes 49156
  232.0 5.8 collective-permute-start
  237.8 5.8 collective-permute-start.1
  243.5 5.8 collective-permute-start.2
  249.9 5.8 collective-permute-start.3
  256.3 5.8 collective-permute-start.4
  262.6 5.8 collective-permute-start.5
  269.0 5.8 collective-permute-start.6
  275.4 5.8 collective-permute-start.7
  281.8 5.8 collective-permute-start.8
  288.1 5.8 collective-permute-start.9
  294.5 5.8 collective-permute-start.10
  300.8 5.8 collective-permute-start.11
  307.2 5.8 collective-permute-start.12
  313.6 5.9 collective-permute-start.13
  319.5 6.1 collective-permute-start.14
  345.8 6.6 collective-permute-start.15
  348.0 13.4 %copy-start.72 = (s32[8]{0:T(128)}, s32[8]{0:T(128)S(1)}, u32[]{:S(2)}) copy-start(s32[8]{0:T(128)S(1)} %iota_add_fusion) | copy-start | bytes 100
  353.5 7.9 copy-start.27
  353.7 7.7 copy-start.74
  354.1 6.5 collective-permute-start.16
  360.6 291.0 %reduce-scatter.22.cloned.1.call-start = ((), (), s32[]{:S(2)}) async-start(), calls=%async_computation.17 | async-start | bytes 417792
  433.0 8.0 copy-start.14
  433.0 8.0 copy-start.10
  433.0 8.0 copy-start.54
  468.2 184.8 %reduce-scatter.20.cloned.1.call-start = ((), (), s32[]{:S(2)}) async-start(), calls=%async_computation.12 | async-start | bytes 1671168 | tf_op jit(solution)/shard_map/reduce_scatter | solution.py:312
  470.0 183.0 %reduce-scatter.14.cloned.1.call-start = ((), (), s32[]{:S(2)}) async-start(), calls=%async_computation.9 | async-start | bytes 2506752 | tf_op jit(solution)/shard_map/reduce_scatter | solution.py:302
  472.7 274.4 %reduce-scatter.12.cloned.1.call-start = ((), (), s32[]{:S(2)}) async-start(), calls=%async_computation.8 | async-start | bytes 7520256 | tf_op jit(solution)/shard_map/reduce_scatter | solution.py:300
  488.8 8.1 copy-start.16
  503.8 358.7 %reduce-scatter.16.cloned.1.call-start = ((), (), s32[]{:S(2)}) async-start(), calls=%async_computation.10 | async-start | bytes 10027008 | tf_op jit(solution)/shard_map/reduce_scatter | solution.py:306
  514.4 464.5 %reduce-scatter.18.cloned.1.call-start = ((), (), s32[]{:S(2)}) async-start(), calls=%async_computation.11 | async-start | bytes 10027008 | tf_op jit(solution)/shard_map/reduce_scatter | solution.py:308
  529.4 47.2 %copy-start.31 = (f32[768]{0:T(1024)S(1)}, f32[768]{0:T(1024)}, u32[]{:S(2)}) copy-start(f32[768]{0:T(1024)} %copy-done.30) | copy-start | bytes 9220
  576.6 6.7 copy-start.9
  (70 other events, 174.9 us)
Sparse Core Ops, SparseCore 0:
  10.3 50.0 all-gather.19
  62.7 38.0 all-gather.21
  103.1 53.6 all-gather.23
  158.8 52.0 all-gather.25
  360.8 52.5 reduce-scatter.9
  468.4 54.6 reduce-scatter.21
  527.7 58.4 reduce-scatter.19
  590.6 62.2 reduce-scatter.13
  658.0 88.9 reduce-scatter.11
  751.6 110.8 reduce-scatter.15
  867.7 111.0 reduce-scatter.17
